TPU v7x, 256 devices: a whole 4x4x8 slice. The times are simulated.
256 devices in a mesh: comp: 2 (over x_lo), ox: 16 (over x_hi, y, core), oy: 8 (over z).
Axes of the slice: x: 4 (x_hi: 2, x_lo: 2; x = x_hi * 2 + x_lo), y: 4, z: 8, core: 2. Of those that a mesh axis runs over, the one named last changes fastest.
Arguments:
- atmos_stress: float32 [2, 2359296], P(None, ('comp', 'ox', 'oy')), may hold values from -6 to 6
- route_tile: int32 [2359296, 1], P(('comp', 'ox', 'oy')), may hold values from 0 to 255; in each aligned block of 9216 rows (0 to 9215, 9216 to 18431, ...) at most 144 rows name the same one
- route_cell: int32 [2359296], P(('comp', 'ox', 'oy')), may hold values from 0 to 54674
- route_weight: float32 [2359296], P(('comp', 'ox', 'oy')), may hold values from 0.25 to 1
- velocity: float32 [2, 8, 4320, 3240], P(None, None, ('comp', 'ox'), 'oy'), may hold values from -6 to 6
- thickness: float32 [8, 4320, 3240], P(None, ('comp', 'ox'), 'oy'), may hold values from 0.5 to 2
- coriolis: float32 [4320, 3240], P(('comp', 'ox'), 'oy'), may hold values from -0.5 to 0.5
- ocean_axes: float32 [2, 3, 4320, 3240], P(None, None, ('comp', 'ox'), 'oy'), may hold values from -3 to 3
- ocean_mask: int32 [4320, 3240], P(('comp', 'ox'), 'oy'), may hold values 0 or 1
Outputs:
- new_velocity: float32 [2, 8, 4320, 3240], P(None, None, ('comp', 'ox'), 'oy')
Inputs may be any that keep to these rules, and one draw needn't show every extreme that they name: `route_tile`: tiles are numbered as devices, comp-major, then ox, then oy. Of the 9216 cells of one device, at most 144 name the same tile, and on some device exactly 144 do.
All inputs are finite; a program needn't handle non-finite values. No bound on the sum of `ocean_mask` on one device may be relied on, other than what follows from the above.
Results may differ from a plain program's by a relative error of at most 0.0003.
Values sent between devices are 32-bit elements; how exact they have to be, the bound alone decides.
A program may use at most 128 MiB of HBM per device.

v0:
```python
import math
import jax
import jax.numpy as jnp
import numpy as np
from jax import lax
from jax.sharding import PartitionSpec as P

A_ROWS = 48
A_COLS = 64
face_normal = np.array(
    [[1.0, 0, 0], [0, 1.0, 0], [-1.0, 0, 0], [0, -1.0, 0], [0, 0, 1.0], [0, 0, -1.0]]
)
face_first = np.array(
    [[0, 1.0, 0], [-1.0, 0, 0], [0, -1.0, 0], [1.0, 0, 0], [0, 1.0, 0], [0, 1.0, 0]]
)
face_second = np.array(
    [[0, 0, 1.0], [0, 0, 1.0], [0, 0, 1.0], [0, 0, 1.0], [-1.0, 0, 0], [1.0, 0, 0]]
)
viscosity = 0.2
coupling = 0.3
bottom_drag = 0.1


def extended(block, sides, width, periodic):
    for axis, dim in sides:
        count = lax.axis_size(axis)
        forward = [(i, i + 1) for i in range(count - 1)]
        if periodic:
            forward.append((count - 1, 0))
        backward = [(target, source) for source, target in forward]
        low = lax.ppermute(
            lax.slice_in_dim(block, block.shape[dim] - width, None, axis=dim), axis, forward
        )
        high = lax.ppermute(lax.slice_in_dim(block, 0, width, axis=dim), axis, backward)
        block = jnp.concatenate([low, block, high], axis=dim)
    return block


def frame_rows(face_table, face_id):
    face_numbers = jnp.arange(6, dtype=jnp.int32)
    face_hits = (face_id[None, :] == face_numbers[:, None]).astype(jnp.float32)
    return jnp.dot(
        jnp.asarray(face_table.T, dtype=jnp.float32), face_hits, precision=lax.Precision.HIGHEST
    )


def tangent(direction, radial):
    projected = direction - jnp.sum(direction * radial, axis=0, keepdims=True) * radial
    return projected / jnp.sqrt(jnp.sum(projected * projected, axis=0, keepdims=True))


def cartesian(stress, face_id, cell_row, cell_col, cube_rows, cube_cols):
    normal = frame_rows(face_normal, face_id)
    first_axis = frame_rows(face_first, face_id)
    second_axis = frame_rows(face_second, face_id)
    slant_row = jnp.tan(
        (cell_row.astype(jnp.float32) + 0.5) * (0.5 * math.pi / cube_rows) - 0.25 * math.pi
    )
    slant_col = jnp.tan(
        (cell_col.astype(jnp.float32) + 0.5) * (0.5 * math.pi / cube_cols) - 0.25 * math.pi
    )
    surface_point = normal + slant_row[None, :] * first_axis + slant_col[None, :] * second_axis
    radial = surface_point / jnp.sqrt(jnp.sum(surface_point * surface_point, axis=0, keepdims=True))
    return stress[0][None, :] * tangent(first_axis, radial) + stress[1][None, :] * tangent(
        second_axis, radial
    )


def advance(masked, east, west, north, south, thickness, coriolis, ocean_stress, sea_mask):
    laplacian = east + west + north + south - 4.0 * masked
    turning = jnp.stack([coriolis * masked[1], -coriolis * masked[0]])
    interface_depth = 0.5 * (thickness[:-1] + thickness[1:])
    inner_flux = coupling * (masked[:, :-1] - masked[:, 1:]) / interface_depth[None]
    fluxes = jnp.concatenate(
        [ocean_stress[:, None], inner_flux, bottom_drag * masked[:, -1:]], axis=1
    )
    vertical = (fluxes[:, :-1] - fluxes[:, 1:]) / thickness[None]
    return (masked + turning + viscosity * laplacian + vertical) * sea_mask


def pack_blocks(payload, target, tile_count, capacity):
    cell_count = target.shape[0]
    block_len = math.gcd(cell_count, 512)
    block_count = cell_count // block_len
    tile_numbers = jnp.arange(tile_count, dtype=jnp.int32)
    hits = (target[:, None] == tile_numbers[None, :]).astype(jnp.float32)
    hit_blocks = hits.reshape(block_count, block_len, tile_count)
    lower = (jnp.arange(block_len)[:, None] > jnp.arange(block_len)[None, :]).astype(jnp.bfloat16)
    within = jnp.einsum(
        "ij,bjt->bit", lower, hit_blocks.astype(jnp.bfloat16), preferred_element_type=jnp.float32
    )
    totals = jnp.sum(hit_blocks, axis=1)
    before = jnp.cumsum(totals, axis=0) - totals
    rank_blocks = jnp.sum((within + before[:, None, :]) * hit_blocks, axis=2)
    payload_blocks = payload.reshape(payload.shape[0], block_count, block_len).transpose(1, 0, 2)
    slot_numbers = jnp.arange(capacity, dtype=jnp.float32)

    def pack_add_block(packed, pieces):
        hit_block, rank_block, payload_block = pieces
        slot_hits = (rank_block[:, None] == slot_numbers[None, :]).astype(jnp.float32)
        spread = payload_block[:, :, None] * hit_block[None, :, :]
        return (
            packed + jnp.einsum("cgt,gs->cts", spread, slot_hits, precision=lax.Precision.HIGHEST),
            None,
        )

    start = jnp.zeros((payload.shape[0], tile_count, capacity), jnp.float32)
    packed, unused = lax.scan(pack_add_block, start, (hit_blocks, rank_blocks, payload_blocks))
    return packed


def unpack_blocks(received, tile_count, capacity, tile_width, tile_depth):
    group = 1
    while group * 2 <= tile_count and group * 2 * capacity <= 2048:
        group = group * 2
    group_count = tile_count // group
    blocks = received.reshape(4, group_count, group * capacity).transpose(1, 0, 2)
    x_numbers = jnp.arange(tile_width, dtype=jnp.int32)
    y_numbers = jnp.arange(tile_depth, dtype=jnp.int32)

    def unpack_add_block(surface, block):
        cell_number = block[3].astype(jnp.int32)
        x_offset = cell_number // tile_depth
        y_offset = cell_number % tile_depth
        x_hits = (x_offset[None, :] == x_numbers[:, None]).astype(jnp.float32)
        y_hits = (y_offset[:, None] == y_numbers[None, :]).astype(jnp.float32)
        spread = (block[:3][:, None, :] * x_hits[None]).reshape(3 * tile_width, -1)
        return (surface + jnp.dot(spread, y_hits, precision=lax.Precision.HIGHEST), None)

    start = jnp.zeros((3 * tile_width, tile_depth), jnp.float32)
    surface, unused = lax.scan(unpack_add_block, start, blocks)
    return surface.reshape(3, tile_width, tile_depth)


def shards(
    atmos_stress,
    route_tile,
    route_cell,
    route_weight,
    velocity,
    thickness,
    coriolis,
    ocean_axes,
    ocean_mask,
):
    cell_count = atmos_stress.shape[1]
    face_block = A_ROWS * A_COLS
    halves = lax.axis_size("comp")
    rows_axis = lax.axis_size("ox")
    cols_axis = lax.axis_size("oy")
    tile_count = halves * rows_axis * cols_axis
    capacity = 4 * cell_count // tile_count
    local_index = jnp.arange(cell_count, dtype=jnp.int32)
    face_id = lax.axis_index("comp") * (cell_count // face_block) + local_index // face_block
    cell_row = lax.axis_index("ox") * A_ROWS + local_index // A_COLS % A_ROWS
    cell_col = lax.axis_index("oy") * A_COLS + local_index % A_COLS
    weighted = (
        cartesian(atmos_stress, face_id, cell_row, cell_col, A_ROWS * rows_axis, A_COLS * cols_axis)
        * route_weight[None, :]
    )
    target = route_tile[:, 0]
    payload = jnp.concatenate([weighted, route_cell.astype(jnp.float32)[None, :]], axis=0)
    packed = pack_blocks(payload, target, tile_count, capacity)
    packed = packed.reshape(4, halves, rows_axis * cols_axis, capacity)
    received = lax.all_to_all(
        lax.all_to_all(packed, "comp", split_axis=1, concat_axis=1, tiled=True),
        ("ox", "oy"),
        split_axis=2,
        concat_axis=2,
        tiled=True,
    )
    tile_width = velocity.shape[2]
    tile_depth = velocity.shape[3]
    surface = unpack_blocks(received.reshape(4, -1), tile_count, capacity, tile_width, tile_depth)
    ocean_stress = jnp.sum(ocean_axes * surface[None], axis=1)
    sea_mask = ocean_mask.astype(jnp.float32)
    masked = velocity * sea_mask
    x_rims = extended(masked, ((("comp", "ox"), 2),), 1, True)
    y_rims = extended(masked, (("oy", 3),), 1, False)
    top_row = masked[:, :, :, -1]
    position = lax.axis_index("comp") * rows_axis + lax.axis_index("ox")
    whole_row = lax.all_gather(top_row, ("comp", "ox"), axis=2, tiled=True)
    mirrored = whole_row[:, :, ::-1]
    folded = lax.dynamic_slice_in_dim(mirrored, position * tile_width, tile_width, 2)
    at_fold = lax.axis_index("oy") == cols_axis - 1
    north_rim = jnp.where(at_fold, -folded, y_rims[:, :, :, -1])
    east = x_rims[:, :, 2:, :]
    west = x_rims[:, :, :-2, :]
    north = jnp.concatenate([y_rims[:, :, :, 2:-1], north_rim[:, :, :, None]], axis=3)
    south = y_rims[:, :, :, :-2]
    return advance(masked, east, west, north, south, thickness, coriolis, ocean_stress, sea_mask)


def solution(mesh):
    return jax.shard_map(
        shards,
        mesh=mesh,
        in_specs=(
            P(None, ("comp", "ox", "oy")),
            P(("comp", "ox", "oy"), None),
            P(("comp", "ox", "oy")),
            P(("comp", "ox", "oy")),
            P(None, None, ("comp", "ox"), "oy"),
            P(None, ("comp", "ox"), "oy"),
            P(("comp", "ox"), "oy"),
            P(None, None, ("comp", "ox"), "oy"),
            P(("comp", "ox"), "oy"),
        ),
        out_specs=P(None, None, ("comp", "ox"), "oy"),
        check_vma=False,
    )
```

profile of v0, /device:TPU:1, one launch (start us, length us, event | category | flops | bytes accessed | tf_op | source)
XLA Modules:
  0.0 483.1 jit_solution(10987998646943046107)
XLA Ops:
  3.1 4.8 %fusion.23 = f32[18,512,256]{1,2,0:T(8,128)} fusion(s32[18,512]{1,0:T(8,128)S(1)} %eq.115), kind=kLoop, calls=%fused_computation.36 | loop fusion | flops 4718592 | bytes 9474048 | tf_op jit(solution)/shard_map/convert_element_type | solution.py:86
  9.9 3.8 fusion.22
  14.1 45.8 %while.24 = (s32[]{:T(128)}, f32[4,256,144]{1,2,0:T(8,128)S(1)}, f32[18,4,512]{2,1,0:T(4,128)S(1)}, f32[18,512,256]{1,2,0:T(8,128)}, f32[18,512]{1,0:T(8,128)S(1)}, /*index=5*/s32[]{:T(128)}, s32[]{:T(128)}) while((s32[]{:T(128)}, f32[4,256,144]{1,2,0:T(8,128)S(1)}, f32[18,4,512]{2,1,0:T(4,128)S(1)}, f32[18,512,256]{1,2,0:T(8,128)}, ...), condition=%wide.region_9.10_spmd.clone, body=%wide.region_8.9_spmd.clone.sunk | while | flops 906862592 | bytes 3831907 | solution.py:108
  64.5 8.8 %copy.50 = f32[2,8,135,405]{2,1,0,3:T(8,128)} copy(f32[2,8,135,405]{3,1,2,0:T(8,128)} %param.20) | data formatting | bytes 6998400 | tf_op args[4]
  73.3 3.9 broadcast_multiply_fusion.1
  79.1 5.6 %collective-permute-start.3 = (f32[2,8,135,1]{2,1,0,3:T(8,128)S(1)}, f32[2,8,135,1]{2,1,0,3:T(8,128)}, u32[]{:S(2)}, u32[]{:S(2)}) collective-permute-start(f32[2,8,135,1]{2,1,0,3:T(8,128)S(1)} %get-tuple-element.195), channel_id=1, source_target_pairs={{0,1},{1,2},{2,3},{3,4},{4,5},{5,6},{6,7},{8,9},{9,10},{10,11},{11... | collective-permute-start | bytes 25928 | tf_op jit(solution)/shard_map/ppermute | solution.py:31
  84.7 4.0 fusion.75
  99.1 4.7 copy.66
  103.8 9.4 %fusion.27 = f32[2,7,135,405]{2,1,0,3:T(8,128)} fusion(f32[2,8,135,405]{2,1,0,3:T(8,128)} %copy-done, f32[7,135,405]{1,0,2:T(8,128)} %copy.66), kind=kLoop, calls=%fused_computation.41 | loop fusion | flops 2296350 | bytes 10716300 | tf_op jit(solution)/shard_map/div | solution.py:73
  116.4 15.2 %all-to-all-start.1 = ((f32[4,2,128,144]{3,1,0,2:T(2,128)}), f32[4,2,128,144]{3,1,0,2:T(2,128)S(1)}, u32[]{:S(2)}, u32[]{:S(2)}) async-start(f32[4,2,128,144]{3,1,0,2:T(2,128)} %copy.62), calls=%async_computation.1 | async-start | bytes 2097152 | tf_op jit(solution)/shard_map/all_to_all | solution.py:165
  131.5 6.5 %slice_multiply_fusion.1 = (f32[1,8,135,405]{2,1,0,3:T(8,128)}, f32[1,8,135,405]{2,1,0,3:T(8,128)}) fusion(f32[2,8,135,405]{2,1,0,3:T(8,128)} %copy-done, f32[135,405]{0,1:T(8,128)} %copy.51, f32[135,405]{0,1:T(8,128)} %copy.52), kind=kLoop, calls=%fused_computation.59 | loop fusion | flops 874800 | bytes 7435800 | tf_op jit(solution)/shard_map/mul | solution.py:71
  138.2 4.8 slice_multiply_fusion.2
  143.0 62.0 %all-gather = f32[2,8,4320,1]{1,0,3,2:T(2,128)} all-gather(f32[2,8,135,1]{1,0,3,2:T(2,128)S(1)} %copy.57), channel_id=2, replica_groups=mesh['comp'=2,'ox'=16,'oy'=8] {'comp','ox'}, dimensions={2}, use_global_device_ids=true | all-gather | bytes 285120 | tf_op jit(solution)/shard_map/all_gather | solution.py:182
  204.9 6.4 %slice.95 = f32[2,8,135,404]{2,1,0,3:T(8,128)} slice(f32[2,8,135,405]{2,1,0,3:T(8,128)} %copy-done), slice={[0:2], [0:8], [0:135], [1:405]} | slice | bytes 6981120 | tf_op jit(solution)/shard_map/slice | solution.py:189
  214.6 5.2 %copy.58 = f32[2,8,4320,1]{2,1,0,3:T(8,128)S(1)} copy(f32[2,8,4320,1]{1,0,3,2:T(2,128)} %all-gather) | data formatting | bytes 552960 | tf_op jit(solution)/shard_map/all_gather | solution.py:182
  229.0 206.2 %while.25 = (s32[]{:T(128)}, f32[405,405]{1,0:T(8,128)}, f32[32,4,1152]{2,0,1:T(8,128)S(1)}, s32[]{:T(128)}, s32[]{:T(128)}, /*index=5*/s32[]{}) while((s32[]{:T(128)}, f32[405,405]{1,0:T(8,128)}, f32[32,4,1152]{2,0,1:T(8,128)S(1)}, s32[]{:T(128)}, s32[]{:T(128)}, /*index=5*/s32[]{}) %tuple.73), condition=%wide.region_11.12_spmd.clone, body=%wide.region_10.11_spmd.clone.sunk | while | flops 2269070080 | bytes 15387791 | solution.py:131
  237.3 3.7 fusion.93
  250.2 3.7 fusion.93
  263.1 3.7 fusion.93
  276.0 3.7 fusion.93
  301.7 3.7 fusion.93
  437.5 4.1 multiply_reduce_fusion
  445.0 29.2 %fusion.33 = f32[2,8,135,405]{2,1,0,3:T(8,128)} fusion(f32[2,8,135,405]{2,1,0,3:T(8,128)} %copy-done, f32[2,8,135,1]{2,1,0,3:T(8,128)} %collective-permute-done.3, f32[2,8,1,405]{2,1,0,3:T(8,128)} %copy.56, f32[2,8,1,405]{2,1,0,3:T(8,128)S(1)} %copy-done.2, f32[1,8,135,405]{2,1,0,3:T(8,128)} %get-tuple-element.197, ...), kind=kLoop, calls=%fused_computation.48 | loop fusion | flops 16621200 | bytes 19962180 | tf_op jit(solution)/shard_map/mul | solution.py:78
  474.2 8.8 %copy.69 = f32[2,8,135,405]{3,1,2,0:T(8,128)} copy(f32[2,8,135,405]{2,1,0,3:T(8,128)} %fusion.33) | data formatting | bytes 6998400 | tf_op jit(solution)/shard_map/mul | solution.py:78
  (580 shorter events, 273.9 us)
Async XLA Ops:
  0.0 7.9 %copy-start.13 = (f32[3,6]{1,0:T(4,128)S(1)}, f32[3,6]{1,0:T(4,128)}, u32[]{:S(2)}) copy-start(f32[3,6]{1,0:T(4,128)} %constant.156.clone) | copy-start | bytes 220
  0.0 8.2 %copy-start.12 = (f32[3,6]{1,0:T(4,128)S(1)}, f32[3,6]{1,0:T(4,128)}, u32[]{:S(2)}) copy-start(f32[3,6]{1,0:T(4,128)} %constant.155.clone) | copy-start | bytes 220
  0.0 8.8 %copy-start.11 = (f32[3,6]{1,0:T(4,128)S(1)}, f32[3,6]{1,0:T(4,128)}, u32[]{:S(2)}) copy-start(f32[3,6]{1,0:T(4,128)} %constant.154.clone) | copy-start | bytes 220
  0.0 9.8 %copy-start.8 = (f32[2,9216]{1,0:T(2,128)S(1)}, f32[2,9216]{1,0:T(2,128)}, u32[]{:S(2)}) copy-start(f32[2,9216]{1,0:T(2,128)} %param.16) | copy-start | bytes 221188
  0.0 9.8 %copy-start.10 = (s32[9216]{0:T(1024)S(1)}, s32[9216]{0:T(1024)}, u32[]{:S(2)}) copy-start(s32[9216]{0:T(1024)} %param.18) | copy-start | bytes 110596
  9.9 3.9 copy-start.9
  14.1 50.2 %copy-start.7 = (s32[135,405]{1,0:T(8,128)S(1)}, s32[135,405]{1,0:T(8,128)}, u32[]{:S(2)}) copy-start(s32[135,405]{1,0:T(8,128)} %param.24) | copy-start | bytes 656104
  60.8 54.3 %all-to-all-start = ((f32[4,2,128,144]{2,3,0,1:T(8,128)}), f32[4,2,128,144]{2,3,0,1:T(8,128)S(1)}, u32[]{:S(2)}, u32[]{:S(2)}) async-start(f32[4,2,128,144]{2,3,0,1:T(8,128)} %copy_bitcast_fusion.1), calls=%async_computation | async-start | bytes 1179648 | tf_op jit(solution)/shard_map/all_to_all | solution.py:166
  64.5 12.7 %copy-start.3 = (f32[135,405]{0,1:T(8,128)}, f32[135,405]{0,1:T(8,128)S(1)}, u32[]{:S(2)}) copy-start(f32[135,405]{0,1:T(8,128)S(1)} %copy.49) | copy-start | bytes 656104
  77.2 11.5 %copy-start = (f32[2,8,135,405]{2,1,0,3:T(8,128)}, f32[2,8,135,405]{2,1,0,3:T(8,128)S(1)}, u32[]{:S(2)}) copy-start(f32[2,8,135,405]{2,1,0,3:T(8,128)S(1)} %broadcast_multiply_fusion.1) | copy-start | bytes 10497604
  77.9 144.6 %collective-permute-start.2 = (f32[2,8,135,1]{2,1,0,3:T(8,128)}, f32[2,8,135,1]{2,1,0,3:T(8,128)}, u32[]{:S(2)}, u32[]{:S(2)}) collective-permute-start(f32[2,8,135,1]{2,1,0,3:T(8,128)} %get-tuple-element.194), channel_id=1, source_target_pairs={{1,0},{2,1},{3,2},{4,3},{5,4},{6,5},{7,6},{9,8},{10,9},{11,10},{12... | collective-permute-start | bytes 25928 | tf_op jit(solution)/shard_map/ppermute | solution.py:34
  79.1 365.9 %collective-permute-start.3 = (f32[2,8,135,1]{2,1,0,3:T(8,128)S(1)}, f32[2,8,135,1]{2,1,0,3:T(8,128)}, u32[]{:S(2)}, u32[]{:S(2)}) collective-permute-start(f32[2,8,135,1]{2,1,0,3:T(8,128)S(1)} %get-tuple-element.195), channel_id=1, source_target_pairs={{0,1},{1,2},{2,3},{3,4},{4,5},{5,6},{6,7},{8,9},{9,10},{10,11},{11... | collective-permute-start | bytes 25928 | tf_op jit(solution)/shard_map/ppermute | solution.py:31
  88.7 8.6 %copy-start.1 = (f32[8,135,405]{2,0,1:T(8,128)S(1)}, f32[8,135,405]{2,0,1:T(8,128)}, u32[]{:S(2)}) copy-start(f32[8,135,405]{2,0,1:T(8,128)} %param.21) | copy-start | bytes 5248804
  91.6 131.6 %collective-permute-start = (f32[2,8,1,405]{3,1,2,0:T(8,128)S(1)}, f32[2,8,1,405]{3,1,2,0:T(8,128)S(1)}, u32[]{:S(2)}, u32[]{:S(2)}) collective-permute-start(f32[2,8,1,405]{3,1,2,0:T(8,128)S(1)} %copy.53), channel_id=1, source_target_pairs={{8,0},{16,8},{24,16},{32,24},{40,32},{48,40},{56,48},{64,56},{72,6... | collective-permute-start | bytes 77768 | tf_op jit(solution)/shard_map/ppermute | solution.py:34
  97.3 128.5 %collective-permute-start.1 = (f32[2,8,1,405]{3,1,2,0:T(8,128)S(1)}, f32[2,8,1,405]{3,1,2,0:T(8,128)S(1)}, u32[]{:S(2)}, u32[]{:S(2)}) collective-permute-start(f32[2,8,1,405]{3,1,2,0:T(8,128)S(1)} %copy.55), channel_id=1, source_target_pairs={{0,8},{8,16},{16,24},{24,32},{32,40},{40,48},{48,56},{56,64},{64,7... | collective-permute-start | bytes 77768 | tf_op jit(solution)/shard_map/ppermute | solution.py:31
  103.8 9.4 %copy-start.4 = (f32[135,405]{1,0:T(8,128)S(1)}, f32[135,405]{1,0:T(8,128)}, u32[]{:S(2)}) copy-start(f32[135,405]{1,0:T(8,128)} %param.22) | copy-start | bytes 656104
  116.4 111.9 %all-to-all-start.1 = ((f32[4,2,128,144]{3,1,0,2:T(2,128)}), f32[4,2,128,144]{3,1,0,2:T(2,128)S(1)}, u32[]{:S(2)}, u32[]{:S(2)}) async-start(f32[4,2,128,144]{3,1,0,2:T(2,128)} %copy.62), calls=%async_computation.1 | async-start | bytes 2097152 | tf_op jit(solution)/shard_map/all_to_all | solution.py:165
  229.1 1.8 copy-start.5
  235.5 1.8 copy-start.5
  242.0 1.8 copy-start.5
  248.4 1.8 copy-start.5
  254.8 1.8 copy-start.5
  261.3 1.8 copy-start.5
  435.2 9.8 %copy-start.2 = (f32[2,8,1,405]{2,1,0,3:T(8,128)S(1)}, f32[2,8,1,405]{2,1,0,3:T(8,128)}, u32[]{:S(2)}) copy-start(f32[2,8,1,405]{2,1,0,3:T(8,128)} %copy.54) | copy-start | bytes 77764
  (58 other events, 75.7 us)
where the time goes:
time: 486 us; the launch traced here: 483 us
  local copies, waits for them, and re-layouts  166 us (34%)
  matrix products  145 us (30%)
  other arithmetic  77.8 us (16%)
  blocking collectives  62 us (13%)
  starting transfers between devices  28.6 us (6%)
    dot_general x32, matrix products, unpack_add_block(): jnp.dot(spread, y_hits, precision=lax.Precision.HIGHEST)  119 us
    all_gather x1, blocking collectives, shards(): whole_row = lax.all_gather(top_row, ('comp', 'ox'), axis=2, tiled=True)  62 us
    mul x32, local copies, waits for them, and re-layouts, unpack_add_block(): spread = (block[:3][:, None, :] * x_hits[None]).reshape(3 * tile_width, -1)  46.6 us
    mul x1, other arithmetic, advance(): return (masked + turning + viscosity * laplacian + vertical) * sea_mask  29.2 us
    while x160, local copies, waits for them, and re-layouts  28.7 us
    dynamic_slice x54, local copies, waits for them, and re-layouts, pack_blocks(): lax.scan(pack_add_block, start, (hit_blocks, rank_blocks, payload_blocks))  23.2 us
    dot_general x18, matrix products, pack_add_block(): jnp.einsum('cgt,gs->cts', spread, slot_hits, precision=lax.Precision.HIGH...  21.4 us
    unnamed x30, local copies, waits for them, and re-layouts  16.1 us
  transfers between devices with their start and end apart: 6, of which 0 were waited for; matrix products, arithmetic and copies ran while one was open for 54% of the time, Pallas kernels for 0%

commit v1 on v0

--- a/solution.py
+++ b/solution.py
@@ -179,7 +179,7 @@
     y_rims = extended(masked, (("oy", 3),), 1, False)
     top_row = masked[:, :, :, -1]
     position = lax.axis_index("comp") * rows_axis + lax.axis_index("ox")
-    whole_row = lax.all_gather(top_row, ("comp", "ox"), axis=2, tiled=True)
+    whole_row = jnp.concatenate(lax.all_gather(top_row, ("comp", "ox")), axis=2)
     mirrored = whole_row[:, :, ::-1]
     folded = lax.dynamic_slice_in_dim(mirrored, position * tile_width, tile_width, 2)
     at_fold = lax.axis_index("oy") == cols_axis - 1

time: 486 us -> 466 us (0.959)
  blocking collectives: 62 us -> 47.3 us
  local copies, waits for them, and re-layouts: 166 us -> 161 us
    all_gather x1, blocking collectives: 62 us -> 47.3 us  [shards(): whole_row = jnp.concatenate(lax.all_gather(top_row, ('comp', 'ox')), axis=2)]
    all_gather x1 -> x0, local copies, waits for them, and re-layouts: 5.21 us -> none  [shards(): whole_row = lax.all_gather(top_row, ('comp', 'ox'), axis=2, tiled=True)]
  transfers between devices with their start and end apart: 6 -> 6, of which waited for: 0 -> 0; matrix products, arithmetic and copies ran while one was open for 54% -> 56% of each run, Pallas kernels for 0% -> 0%
where the time goes in v1:
time: 466 us; the launch traced here: 464 us
  local copies, waits for them, and re-layouts  161 us (35%)
  matrix products  145 us (31%)
  other arithmetic  77.8 us (17%)
  blocking collectives  47.3 us (10%)
  starting transfers between devices  28.6 us (6%)
    dot_general x32, matrix products, unpack_add_block(): jnp.dot(spread, y_hits, precision=lax.Precision.HIGHEST)  119 us
    all_gather x1, blocking collectives, shards(): whole_row = jnp.concatenate(lax.all_gather(top_row, ('comp', 'ox')), axis=2)  47.3 us
    mul x32, local copies, waits for them, and re-layouts, unpack_add_block(): spread = (block[:3][:, None, :] * x_hits[None]).reshape(3 * tile_width, -1)  46.6 us
    mul x1, other arithmetic, advance(): return (masked + turning + viscosity * laplacian + vertical) * sea_mask  29.3 us
    while x160, local copies, waits for them, and re-layouts  28.3 us
    dynamic_slice x54, local copies, waits for them, and re-layouts, pack_blocks(): lax.scan(pack_add_block, start, (hit_blocks, rank_blocks, payload_blocks))  23.2 us
    dot_general x18, matrix products, pack_add_block(): jnp.einsum('cgt,gs->cts', spread, slot_hits, precision=lax.Precision.HIGH...  21.4 us
    unnamed x30, local copies, waits for them, and re-layouts  16.1 us
  transfers between devices with their start and end apart: 6, of which 0 were waited for; matrix products, arithmetic and copies ran while one was open for 56% of the time, Pallas kernels for 0%

profile of v1, /device:TPU:1, one launch (start us, length us, event | category | flops | bytes accessed | tf_op | source)
XLA Modules:
  0.0 463.5 jit_solution(1577804663145840517)
XLA Ops:
  3.1 4.8 %fusion.23 = f32[18,512,256]{1,2,0:T(8,128)} fusion(s32[18,512]{1,0:T(8,128)S(1)} %eq.115), kind=kLoop, calls=%fused_computation.36 | loop fusion | flops 4718592 | bytes 9474048 | tf_op jit(solution)/shard_map/convert_element_type | solution.py:86
  9.9 3.8 fusion.22
  14.1 45.8 %while.24 = (s32[]{:T(128)}, f32[4,256,144]{1,2,0:T(8,128)S(1)}, f32[18,4,512]{2,1,0:T(4,128)S(1)}, f32[18,512,256]{1,2,0:T(8,128)}, f32[18,512]{1,0:T(8,128)S(1)}, /*index=5*/s32[]{:T(128)}, s32[]{:T(128)}) while((s32[]{:T(128)}, f32[4,256,144]{1,2,0:T(8,128)S(1)}, f32[18,4,512]{2,1,0:T(4,128)S(1)}, f32[18,512,256]{1,2,0:T(8,128)}, ...), condition=%wide.region_9.10_spmd.clone, body=%wide.region_8.9_spmd.clone.sunk | while | flops 906862592 | bytes 3831907 | solution.py:108
  64.5 8.8 %copy.51 = f32[2,8,135,405]{2,1,0,3:T(8,128)} copy(f32[2,8,135,405]{3,1,2,0:T(8,128)} %param.20) | data formatting | bytes 6998400 | tf_op args[4]
  73.3 3.9 broadcast_multiply_fusion.1
  78.5 5.0 %collective-permute-start.3 = (f32[2,8,135,1]{2,1,0,3:T(8,128)S(1)}, f32[2,8,135,1]{2,1,0,3:T(8,128)S(1)}, u32[]{:S(2)}, u32[]{:S(2)}) collective-permute-start(f32[2,8,135,1]{2,1,0,3:T(8,128)S(1)} %get-tuple-element.196), channel_id=1, source_target_pairs={{0,1},{1,2},{2,3},{3,4},{4,5},{5,6},{6,7},{8,9},{9,10},{10,11},{11... | collective-permute-start | bytes 25928 | tf_op jit(solution)/shard_map/ppermute | solution.py:31
  83.5 4.0 fusion.74
  97.9 4.7 %copy.67 = f32[7,135,405]{1,0,2:T(8,128)} copy(f32[7,135,405]{2,0,1:T(8,128)} %add_multiply_fusion) | data formatting | bytes 3061800 | tf_op jit(solution)/shard_map/mul | solution.py:72
  102.6 9.4 %fusion.27 = f32[2,7,135,405]{2,1,0,3:T(8,128)} fusion(f32[2,8,135,405]{2,1,0,3:T(8,128)} %copy-done, f32[7,135,405]{1,0,2:T(8,128)} %copy.67), kind=kLoop, calls=%fused_computation.41 | loop fusion | flops 2296350 | bytes 10716300 | tf_op jit(solution)/shard_map/div | solution.py:73
  115.2 15.7 %all-to-all-start.1 = ((f32[4,2,128,144]{3,1,0,2:T(2,128)}), f32[4,2,128,144]{3,1,0,2:T(2,128)S(1)}, u32[]{:S(2)}, u32[]{:S(2)}) async-start(f32[4,2,128,144]{3,1,0,2:T(2,128)} %copy.63), calls=%async_computation.1 | async-start | bytes 2097152 | tf_op jit(solution)/shard_map/all_to_all | solution.py:165
  130.9 6.5 %slice_multiply_fusion.1 = (f32[1,8,135,405]{2,1,0,3:T(8,128)}, f32[1,8,135,405]{2,1,0,3:T(8,128)}) fusion(f32[2,8,135,405]{2,1,0,3:T(8,128)} %copy-done, f32[135,405]{0,1:T(8,128)} %copy.52, f32[135,405]{0,1:T(8,128)} %copy.53), kind=kLoop, calls=%fused_computation.59 | loop fusion | flops 874800 | bytes 7435800 | tf_op jit(solution)/shard_map/mul | solution.py:71
  137.4 4.8 %slice_multiply_fusion.2 = f32[2,1,135,405]{2,1,0,3:T(1,128)} fusion(f32[2,8,135,405]{2,1,0,3:T(8,128)} %copy-done), kind=kLoop, calls=%fused_computation.65 | loop fusion | flops 109350 | bytes 874800 | tf_op jit(solution)/shard_map/mul | solution.py:75
  142.2 47.3 %all-gather = f32[64,8,135,1]{2,1,3,0:T(8,128)} all-gather(f32[2,8,135,1]{2,1,3,0:T(8,128)S(1)} %get-tuple-element.194), channel_id=2, replica_groups=mesh['comp'=2,'ox'=16,'oy'=8] {'comp','ox'}, dimensions={0}, use_global_device_ids=true | all-gather | bytes 285120 | tf_op jit(solution)/shard_map/all_gather | solution.py:182
  189.4 6.4 %slice.95 = f32[2,8,135,404]{2,1,0,3:T(8,128)} slice(f32[2,8,135,405]{2,1,0,3:T(8,128)} %copy-done), slice={[0:2], [0:8], [0:135], [1:405]} | slice | bytes 6981120 | tf_op jit(solution)/shard_map/slice | solution.py:189
  209.9 205.6 %while.25 = (s32[]{:T(128)}, f32[405,405]{1,0:T(8,128)}, f32[32,4,1152]{2,0,1:T(8,128)S(1)}, s32[]{:T(128)}, s32[]{:T(128)}, /*index=5*/s32[]{}) while((s32[]{:T(128)}, f32[405,405]{1,0:T(8,128)}, f32[32,4,1152]{2,0,1:T(8,128)S(1)}, s32[]{:T(128)}, s32[]{:T(128)}, /*index=5*/s32[]{}) %tuple.74), condition=%wide.region_11.12_spmd.clone, body=%wide.region_10.11_spmd.clone.sunk | while | flops 2269070080 | bytes 15387791 | solution.py:131
  211.8 3.7 fusion.92
  218.2 3.7 fusion.92
  224.6 3.7 fusion.92
  263.2 3.7 fusion.92
  346.7 3.7 fusion.92
  385.3 3.7 fusion.92
  417.9 4.1 multiply_reduce_fusion
  425.4 29.3 %fusion.33 = f32[2,8,135,405]{2,1,0,3:T(8,128)} fusion(f32[2,8,135,405]{2,1,0,3:T(8,128)} %copy-done, f32[2,8,135,1]{2,1,0,3:T(8,128)S(1)} %collective-permute-done.3, f32[2,8,1,405]{2,1,0,3:T(8,128)} %copy.57, f32[2,8,1,405]{2,1,0,3:T(8,128)S(1)} %copy-done.2, f32[1,8,135,405]{2,1,0,3:T(8,128)} %get-tuple-element.198, ...), kind=kLoop, calls=%fused_computation.48 | loop fusion | flops 16621200 | bytes 19962180 | tf_op jit(solution)/shard_map/mul | solution.py:78
  454.7 8.8 %copy.70 = f32[2,8,135,405]{3,1,2,0:T(8,128)} copy(f32[2,8,135,405]{2,1,0,3:T(8,128)} %fusion.33) | data formatting | bytes 6998400 | tf_op jit(solution)/shard_map/mul | solution.py:78
  (580 shorter events, 270.5 us)
Async XLA Ops:
  0.0 7.9 %copy-start.13 = (f32[3,6]{1,0:T(4,128)S(1)}, f32[3,6]{1,0:T(4,128)}, u32[]{:S(2)}) copy-start(f32[3,6]{1,0:T(4,128)} %constant.156.clone) | copy-start | bytes 220
  0.0 8.2 %copy-start.12 = (f32[3,6]{1,0:T(4,128)S(1)}, f32[3,6]{1,0:T(4,128)}, u32[]{:S(2)}) copy-start(f32[3,6]{1,0:T(4,128)} %constant.155.clone) | copy-start | bytes 220
  0.0 8.8 %copy-start.11 = (f32[3,6]{1,0:T(4,128)S(1)}, f32[3,6]{1,0:T(4,128)}, u32[]{:S(2)}) copy-start(f32[3,6]{1,0:T(4,128)} %constant.154.clone) | copy-start | bytes 220
  0.0 9.8 %copy-start.8 = (f32[2,9216]{1,0:T(2,128)S(1)}, f32[2,9216]{1,0:T(2,128)}, u32[]{:S(2)}) copy-start(f32[2,9216]{1,0:T(2,128)} %param.16) | copy-start | bytes 221188
  0.0 9.8 %copy-start.10 = (s32[9216]{0:T(1024)S(1)}, s32[9216]{0:T(1024)}, u32[]{:S(2)}) copy-start(s32[9216]{0:T(1024)} %param.18) | copy-start | bytes 110596
  9.9 3.9 copy-start.9
  14.1 50.2 %copy-start.7 = (s32[135,405]{1,0:T(8,128)S(1)}, s32[135,405]{1,0:T(8,128)}, u32[]{:S(2)}) copy-start(s32[135,405]{1,0:T(8,128)} %param.24) | copy-start | bytes 656104
  60.8 53.1 %all-to-all-start = ((f32[4,2,128,144]{2,3,0,1:T(8,128)}), f32[4,2,128,144]{2,3,0,1:T(8,128)S(1)}, u32[]{:S(2)}, u32[]{:S(2)}) async-start(f32[4,2,128,144]{2,3,0,1:T(8,128)} %copy_bitcast_fusion.1), calls=%async_computation | async-start | bytes 1179648 | tf_op jit(solution)/shard_map/all_to_all | solution.py:166
  64.5 12.7 %copy-start.3 = (f32[135,405]{0,1:T(8,128)}, f32[135,405]{0,1:T(8,128)S(1)}, u32[]{:S(2)}) copy-start(f32[135,405]{0,1:T(8,128)S(1)} %copy.50) | copy-start | bytes 656104
  77.2 10.3 %copy-start = (f32[2,8,135,405]{2,1,0,3:T(8,128)}, f32[2,8,135,405]{2,1,0,3:T(8,128)S(1)}, u32[]{:S(2)}) copy-start(f32[2,8,135,405]{2,1,0,3:T(8,128)S(1)} %broadcast_multiply_fusion.1) | copy-start | bytes 10497604
  77.2 126.1 %collective-permute-start.2 = (f32[2,8,135,1]{2,1,0,3:T(8,128)S(1)}, f32[2,8,135,1]{2,1,0,3:T(8,128)}, u32[]{:S(2)}, u32[]{:S(2)}) collective-permute-start(f32[2,8,135,1]{2,1,0,3:T(8,128)S(1)} %get-tuple-element.195), channel_id=1, source_target_pairs={{1,0},{2,1},{3,2},{4,3},{5,4},{6,5},{7,6},{9,8},{10,9},{11,10},{12... | collective-permute-start | bytes 25928 | tf_op jit(solution)/shard_map/ppermute | solution.py:34
  78.5 346.8 %collective-permute-start.3 = (f32[2,8,135,1]{2,1,0,3:T(8,128)S(1)}, f32[2,8,135,1]{2,1,0,3:T(8,128)S(1)}, u32[]{:S(2)}, u32[]{:S(2)}) collective-permute-start(f32[2,8,135,1]{2,1,0,3:T(8,128)S(1)} %get-tuple-element.196), channel_id=1, source_target_pairs={{0,1},{1,2},{2,3},{3,4},{4,5},{5,6},{6,7},{8,9},{9,10},{10,11},{11... | collective-permute-start | bytes 25928 | tf_op jit(solution)/shard_map/ppermute | solution.py:31
  87.5 8.6 %copy-start.1 = (f32[8,135,405]{2,0,1:T(8,128)S(1)}, f32[8,135,405]{2,0,1:T(8,128)}, u32[]{:S(2)}) copy-start(f32[8,135,405]{2,0,1:T(8,128)} %param.21) | copy-start | bytes 5248804
  90.4 113.7 %collective-permute-start = (f32[2,8,1,405]{3,1,2,0:T(8,128)S(1)}, f32[2,8,1,405]{3,1,2,0:T(8,128)S(1)}, u32[]{:S(2)}, u32[]{:S(2)}) collective-permute-start(f32[2,8,1,405]{3,1,2,0:T(8,128)S(1)} %copy.54), channel_id=1, source_target_pairs={{8,0},{16,8},{24,16},{32,24},{40,32},{48,40},{56,48},{64,56},{72,6... | collective-permute-start | bytes 77768 | tf_op jit(solution)/shard_map/ppermute | solution.py:34
  96.1 110.6 %collective-permute-start.1 = (f32[2,8,1,405]{3,1,2,0:T(8,128)S(1)}, f32[2,8,1,405]{3,1,2,0:T(8,128)S(1)}, u32[]{:S(2)}, u32[]{:S(2)}) collective-permute-start(f32[2,8,1,405]{3,1,2,0:T(8,128)S(1)} %copy.56), channel_id=1, source_target_pairs={{0,8},{8,16},{16,24},{24,32},{32,40},{40,48},{48,56},{56,64},{64,7... | collective-permute-start | bytes 77768 | tf_op jit(solution)/shard_map/ppermute | solution.py:31
  102.6 9.4 %copy-start.4 = (f32[135,405]{1,0:T(8,128)S(1)}, f32[135,405]{1,0:T(8,128)}, u32[]{:S(2)}) copy-start(f32[135,405]{1,0:T(8,128)} %param.22) | copy-start | bytes 656104
  115.2 94.0 %all-to-all-start.1 = ((f32[4,2,128,144]{3,1,0,2:T(2,128)}), f32[4,2,128,144]{3,1,0,2:T(2,128)S(1)}, u32[]{:S(2)}, u32[]{:S(2)}) async-start(f32[4,2,128,144]{3,1,0,2:T(2,128)} %copy.63), calls=%async_computation.1 | async-start | bytes 2097152 | tf_op jit(solution)/shard_map/all_to_all | solution.py:165
  210.0 1.8 copy-start.5
  216.4 1.8 copy-start.5
  222.8 1.8 copy-start.5
  229.3 1.8 copy-start.5
  242.1 1.8 copy-start.5
  248.5 1.8 copy-start.5
  415.6 9.8 %copy-start.2 = (f32[2,8,1,405]{2,1,0,3:T(8,128)S(1)}, f32[2,8,1,405]{2,1,0,3:T(8,128)}, u32[]{:S(2)}) copy-start(f32[2,8,1,405]{2,1,0,3:T(8,128)} %copy.55) | copy-start | bytes 77764
  (58 other events, 75.2 us)
